TPU v7x, 32 devices: a whole 2x2x4 slice. The times are simulated.
32 devices in a mesh: ctx: 2 (over y), section: 4 (over x, core), tp: 4 (over z).
Axes of the slice: x: 2, y: 2, z: 4, core: 2. Of those that a mesh axis runs over, the one named last changes fastest.
Arguments:
- queries: bfloat16 [256, 8192], P('ctx', ('section', 'tp')), may hold values from -140 to 140
- keys: bfloat16 [256, 1024], P('ctx', 'section'), may hold values from -6 to 6
- values: bfloat16 [256, 1024], P('ctx', 'section'), may hold values from -36 to 36
- out_grad: bfloat16 [256, 8192], P('ctx', ('section', 'tp')), may hold values from -6 to 6
- enc_weight: bfloat16 [8192, 65536], P(('section', 'tp'), 'ctx'), may hold values from -0.0625 to 0.0625
- enc_bias: float32 [65536], P(('ctx', 'section', 'tp')), may hold values from -3 to 3
- dec_weight: bfloat16 [65536, 8192], P('ctx', ('section', 'tp')), may hold values from -0.0625 to 0.0625
Outputs:
- query_grad: bfloat16 [256, 8192], P('ctx', ('section', 'tp'))
- gradient_keys: bfloat16 [256, 1024], P('ctx', 'section')
- gradient_values: bfloat16 [256, 1024], P('ctx', 'section')
- feature_scores: float32 [65536], P(('ctx', 'section', 'tp'))
All inputs are finite; a program needn't handle non-finite values.
Results may differ from a plain program's by a relative error of at most 0.015.
Values may be sent and summed in bfloat16 or wider, within the bound.
No kernel may reach another device: no remote copies, remote signals or barrier semaphores. Data moves between devices by JAX's collectives and lax.ppermute only.
A program may use at most 256 MiB of HBM per device.

v0:
```python
import math
import jax
import jax.numpy as jnp
from jax import lax
from jax.sharding import PartitionSpec as P

QUERY_HEADS = 64
KEY_VALUE_HEADS = 8
HEAD_SIZE = 128
D_Z = 8192
NEGATIVE = -1e30


def passed_along(value, axis, steps):
    count = lax.axis_size(axis)
    pairs = [(source, (source + steps) % count) for source in range(count)]
    return lax.ppermute(value, axis, pairs)


def spread(value, axis, root):
    mine = lax.axis_index(axis) == root
    return lax.psum(jnp.where(mine, value, jnp.zeros_like(value)), axis)


def token_positions(device, row_count, cycle_size):
    half = row_count // 2
    local = jnp.arange(row_count, dtype=jnp.int32)
    block = jnp.where(local >= half, 2 * cycle_size - 1 - device, device)
    return block * half + local % half


def causal_block(query_pos, anchor, row_count, cycle_size):
    key_pos = token_positions(anchor, row_count, cycle_size)
    return query_pos[:, None] >= key_pos[None, :]


def pass_gradients(key_acc, value_acc):
    return passed_along((key_acc, value_acc), "ctx", -1)


def body(queries, keys, values, out_grad, enc_weight, enc_bias, dec_weight):
    row_count = queries.shape[0]
    heads_here = queries.shape[1] // HEAD_SIZE
    kv_here = keys.shape[1] // HEAD_SIZE
    group_width = QUERY_HEADS // KEY_VALUE_HEADS
    score_scale = 1.0 / math.sqrt(HEAD_SIZE)
    cycle_size = lax.axis_size("ctx")
    cycle_index = lax.axis_index("ctx")
    local_kv = lax.axis_index("tp") * heads_here // group_width
    key_own = lax.dynamic_slice_in_dim(keys, local_kv * HEAD_SIZE, HEAD_SIZE, 1)
    value_own = lax.dynamic_slice_in_dim(values, local_kv * HEAD_SIZE, HEAD_SIZE, 1)
    query_heads = queries.reshape(row_count, heads_here, HEAD_SIZE)
    grad_heads = out_grad.reshape(row_count, heads_here, HEAD_SIZE)
    query_pos = token_positions(cycle_index, row_count, cycle_size)
    store_count = 1

    def block_logits(turn, key_blk):
        anchor = (cycle_index + turn) % cycle_size
        causal_mask = causal_block(query_pos, anchor, row_count, cycle_size)
        logits = (
            jnp.einsum("qhd,kd->hqk", query_heads, key_blk, preferred_element_type=jnp.float32)
            * score_scale
        )
        return (causal_mask, logits)

    def forward_turn(turn, loop_state):
        key_blk, value_blk, running_max, running_sum, running_out, key_store, value_store = (
            loop_state
        )
        causal_mask, logits = block_logits(turn, key_blk)
        logits = jnp.where(causal_mask[None], logits, NEGATIVE)
        new_max = jnp.maximum(running_max, jnp.max(logits, axis=2))
        weights = jnp.where(causal_mask[None], jnp.exp(logits - new_max[:, :, None]), 0.0)
        factor = jnp.exp(running_max - new_max)
        running_sum = running_sum * factor + jnp.sum(weights, axis=2)
        weights_high = weights.astype(jnp.bfloat16)
        weights_low = (weights - weights_high.astype(jnp.float32)).astype(jnp.bfloat16)
        block_out = jnp.einsum(
            "hqk,kd->hqd", weights_high, value_blk, preferred_element_type=jnp.float32
        )
        block_out = block_out + jnp.einsum(
            "hqk,kd->hqd", weights_low, value_blk, preferred_element_type=jnp.float32
        )
        running_out = running_out * factor[:, :, None] + block_out
        key_blk, value_blk = passed_along((key_blk, value_blk), "ctx", -1)
        return (key_blk, value_blk, new_max, running_sum, running_out, key_store, value_store)

    empty_store = jnp.zeros((store_count, row_count, HEAD_SIZE), jnp.bfloat16)
    start_state = (
        key_own,
        value_own,
        jnp.full((heads_here, row_count), NEGATIVE, jnp.float32),
        jnp.zeros((heads_here, row_count), jnp.float32),
        jnp.zeros((heads_here, row_count, HEAD_SIZE), jnp.float32),
        empty_store,
        empty_store,
    )
    final_state = lax.fori_loop(0, cycle_size, forward_turn, start_state)
    running_max, running_sum, running_out, key_store, value_store = final_state[2:]
    log_total = running_max + jnp.log(running_sum)
    head_out = jnp.transpose(
        (running_out / running_sum[:, :, None]).astype(jnp.bfloat16), (1, 0, 2)
    )
    attn_flat = head_out.reshape(row_count, heads_here * HEAD_SIZE)
    row_dots = jnp.sum(grad_heads.astype(jnp.float32) * head_out.astype(jnp.float32), axis=2).T

    def gradient_terms(turn, key_blk, value_blk):
        causal_mask, logits = block_logits(turn, key_blk)
        weights = jnp.where(causal_mask[None], jnp.exp(logits - log_total[:, :, None]), 0.0)
        value_term = jnp.einsum(
            "hqk,qhd->kd",
            weights.astype(jnp.bfloat16),
            grad_heads,
            preferred_element_type=jnp.float32,
        )
        weight_grad = jnp.einsum(
            "qhd,kd->hqk", grad_heads, value_blk, preferred_element_type=jnp.float32
        )
        logit_half = (weights * (weight_grad - row_dots[:, :, None])).astype(jnp.bfloat16)
        query_term = jnp.einsum(
            "hqk,kd->qhd", logit_half, key_blk, preferred_element_type=jnp.float32
        )
        key_term = jnp.einsum(
            "hqk,qhd->kd", logit_half, query_heads, preferred_element_type=jnp.float32
        )
        return (query_term, key_term, value_term)

    zero_block = jnp.zeros((row_count, HEAD_SIZE), jnp.float32)
    zero_query = jnp.zeros((row_count, heads_here, HEAD_SIZE), jnp.float32)

    def moving_turn(turn, loop_state):
        key_blk, value_blk, key_acc, value_acc, query_acc = loop_state
        query_term, key_term, value_term = gradient_terms(turn, key_blk, value_blk)
        key_blk, value_blk = passed_along((key_blk, value_blk), "ctx", -1)
        key_acc, value_acc = pass_gradients(key_acc + key_term, value_acc + value_term)
        return (key_blk, value_blk, key_acc, value_acc, query_acc + query_term)

    moved_state = lax.fori_loop(
        0, cycle_size, moving_turn, (key_own, value_own, zero_block, zero_block, zero_query)
    )
    key_acc, value_acc, query_acc = moved_state[2:]
    query_grad = (
        (query_acc * score_scale).reshape(row_count, heads_here * HEAD_SIZE).astype(jnp.bfloat16)
    )
    head_slot = (jnp.arange(kv_here, dtype=jnp.int32) == local_kv)[None, :, None]
    key_full = jnp.where(head_slot, (key_acc * score_scale)[:, None, :], 0.0).reshape(
        row_count, kv_here * HEAD_SIZE
    )
    value_full = jnp.where(head_slot, value_acc[:, None, :], 0.0).reshape(
        row_count, kv_here * HEAD_SIZE
    )
    key_sum, value_sum = lax.psum((key_full, value_full), "tp")
    last_index = cycle_size - 1
    scored_out, scored_grad = (
        spread(attn_flat, "ctx", last_index),
        spread(out_grad, "ctx", last_index),
    )
    wide_out = scored_out.astype(jnp.float32)
    squares = lax.psum(jnp.sum(wide_out * wide_out, axis=1), ("section", "tp"))
    row_norm = jnp.sqrt(squares / D_Z + 1e-06)
    encoded_part = jnp.dot(scored_out, enc_weight, preferred_element_type=jnp.float32)
    attrib_part = lax.dot_general(
        scored_grad, dec_weight, (((1,), (1,)), ((), ())), preferred_element_type=jnp.float32
    )
    encoded, attrib = (
        lax.psum_scatter(encoded_part, ("section", "tp"), scatter_dimension=1, tiled=True),
        lax.psum_scatter(attrib_part, ("section", "tp"), scatter_dimension=1, tiled=True),
    )
    active = jnp.maximum(encoded / row_norm[:, None] + enc_bias[None, :], 0.0)
    feature_scores = jnp.sum(active * attrib, axis=0)
    return (
        query_grad,
        key_sum.astype(jnp.bfloat16),
        value_sum.astype(jnp.bfloat16),
        feature_scores,
    )


def solution(mesh):
    placed = (
        P("ctx", ("section", "tp")),
        P("ctx", "section"),
        P("ctx", "section"),
        P("ctx", ("section", "tp")),
        P(("section", "tp"), "ctx"),
        P(("ctx", "section", "tp")),
        P("ctx", ("section", "tp")),
    )
    return jax.shard_map(
        body,
        mesh=mesh,
        in_specs=placed,
        out_specs=(
            P("ctx", ("section", "tp")),
            P("ctx", "section"),
            P("ctx", "section"),
            P(("ctx", "section", "tp")),
        ),
        check_vma=False,
    )
```

profile of v0, /device:TPU:0, one launch (start us, length us, event | category | flops | bytes accessed | tf_op | source)
XLA Modules:
  0.0 448.3 jit_solution(17951976722139428715)
XLA Ops:
  7.3 0.8 constant_dynamic-slice_fusion
  8.1 1.0 copy.18
  9.1 0.1 copy.22
  9.2 11.2 %while.54 = (s32[]{:T(128)}, bf16[128,128]{1,0:T(8,128)(2,1)S(1)}, bf16[128,128]{1,0:T(8,128)(2,1)S(1)}, f32[4,128]{1,0:T(4,128)S(1)}, f32[4,128]{1,0:T(4,128)S(...) while((s32[]{:T(128)}, bf16[128,128]{1,0:T(8,128)(2,1)S(1)}, ...), condition=%wide.region_3.4_spmd.clone.clone.clone, body=%wide.region_0.3_spmd.clone.clone.clone.sunk | while | flops 51598352 | bytes 2838894 | solution.py:98
  9.3 3.0 collective-permute-start
  12.3 0.1 collective-permute-start.1
  12.4 0.1 broadcast_compare_fusion.4
  12.5 0.2 fusion.96
  12.7 0.1 fusion.97
  12.8 0.2 fusion.99
  13.0 0.3 fusion.100
  13.3 0.9 collective-permute-done
  14.2 2.0 collective-permute-done.1
  16.2 0.3 collective-permute-start
  16.6 1.7 collective-permute-start.1
  18.3 0.1 broadcast_compare_fusion.4
  18.4 0.2 fusion.96
  18.6 0.1 fusion.97
  18.7 0.2 fusion.99
  18.9 0.3 fusion.100
  19.2 1.0 collective-permute-done
  20.1 0.4 collective-permute-done.1
  20.5 0.1 copy.21
  20.6 0.7 broadcast_select_fusion
  21.3 0.7 broadcast_select_fusion.1
  22.1 25.8 %all-reduce.5.cloned.1.call-done = (bf16[128,512]{1,0:T(8,128)(2,1)}, bf16[128,512]{0,1:T(8,128)(2,1)}) async-done(((bf16[128,512]{1,0:T(8,128)(2,1)}, bf16[128,512]{0,1:T(8,128)(2,1)}), (bf16[128,512]{1,0:T(8,128)(2,1)}, bf16[128,512]{0,1:T(8,128)(2,1)})) %all-reduce.5.cloned.1.call-update) | async-done | bytes 262160 | tf_op jit(solution)/shard_map/psum | solution.py:22
  47.8 21.1 %fusion.48 = f32[128,32768]{1,0:T(8,128)} fusion(bf16[128,512]{0,1:T(8,128)(2,1)} %get-tuple-element.839, bf16[512,32768]{1,0:T(8,128)(2,1)} %param.15), kind=kOutput, calls=%fused_computation.83 | convolution fusion | flops 4294967296 | bytes 50462720 | tf_op jit(solution)/shard_map/dot_general | solution.py:161
  69.1 24.8 %fusion.49 = f32[128,32768]{1,0:T(8,128)} fusion(bf16[128,512]{1,0:T(8,128)(2,1)S(1)} %copy-done.2, bf16[32768,512]{1,0:T(8,128)(2,1)} %param.17), kind=kOutput, calls=%fused_computation.84 | convolution fusion | flops 4294967296 | bytes 50462720 | tf_op jit(solution)/shard_map/dot_general | solution.py:162
  93.9 0.1 copy.20
  94.0 0.1 copy.23
  94.2 0.1 broadcast_bitcast_fusion
  94.3 16.7 %while.55 = (s32[]{:T(128)}, bf16[128,128]{1,0:T(8,128)(2,1)S(1)}, bf16[128,128]{1,0:T(8,128)(2,1)S(1)}, f32[128,128]{1,0:T(8,128)S(1)}, f32[128,128]{1,0:T(8,12...) while((s32[]{:T(128)}, bf16[128,128]{1,0:T(8,128)(2,1)S(1)}, ...), condition=%wide.region_6.7_spmd.clone.clone.clone, body=%wide.region_5.6_spmd.clone.clone.clone.sunk | while | flops 84527632 | bytes 3545556 | solution.py:138
  94.3 0.2 collective-permute-start.3
  94.6 1.9 collective-permute-start.2
  96.4 0.1 broadcast_compare_fusion.5
  96.5 0.2 fusion.113
  96.7 0.2 fusion.114
  96.9 0.2 fusion.115
  97.1 0.2 collective-permute-start.4
  97.4 0.2 fusion.116
  97.5 1.9 collective-permute-start.5
  99.5 0.2 fusion.117
  99.7 1.7 collective-permute-done.4
  101.5 0.7 collective-permute-done.5
  102.2 1.6 collective-permute-start.3
  103.7 0.5 collective-permute-start.2
  104.2 0.1 broadcast_compare_fusion.5
  104.3 0.2 fusion.113
  104.5 0.2 fusion.114
  104.7 0.2 fusion.115
  104.9 1.6 collective-permute-start.4
  106.5 0.2 fusion.116
  106.7 0.5 collective-permute-start.5
  107.2 0.2 fusion.117
  107.5 0.2 collective-permute-done.2
  107.7 1.6 collective-permute-done.4
  109.2 1.8 collective-permute-done.5
  111.2 33.0 %all-reduce.6 = (bf16[128,256]{1,0:T(8,128)(2,1)}, bf16[128,256]{1,0:T(8,128)(2,1)}) all-reduce(f32[128,256]{1,0:T(8,128)S(1)} %get-tuple-element.845, f32[128,256]{1,0:T(8,128)S(1)} %get-tuple-element.844), channel_id=1, replica_groups=mesh['ctx'=2,'section'=4,'tp'=4] {'tp'}, use_global_device_ids=true, to_apply=%region_7.8 | all-reduce | flops 65536 | bytes 393216 | tf_op jit(solution)/shard_map/psum | solution.py:152
  144.3 0.7 copy_bitcast_fusion
  144.9 0.1 multiply_reduce_fusion.1
  145.0 32.5 %psum.38 = f32[128]{0:T(128)S(1)} all-reduce(f32[128]{0:T(128)S(1)} %multiply_reduce_fusion.1), channel_id=1, replica_groups=mesh['ctx'=2,'section'=4,'tp'=4] {'section','tp'}, use_global_device_ids=true, to_apply=%region_12.13 | all-reduce | flops 128 | bytes 1024 | tf_op jit(solution)/shard_map/psum | solution.py:159
  177.5 79.6 %reduce-scatter.3.cloned.1.call-done = f32[128,2048]{1,0:T(8,128)} async-done(((f32[128,32768]{1,0:T(8,128)}), f32[128,2048]{1,0:T(8,128)}) %reduce-scatter.3.cloned.1.call-update) | async-done | bytes 1048592 | tf_op jit(solution)/shard_map/reduce_scatter | solution.py:166
  257.1 182.2 %reduce-scatter.5.cloned.1.call-done = f32[128,2048]{1,0:T(8,128)} async-done(((f32[128,32768]{1,0:T(8,128)}), f32[128,2048]{1,0:T(8,128)}) %reduce-scatter.5.cloned.1.call-update) | async-done | bytes 1048592 | tf_op jit(solution)/shard_map/reduce_scatter | solution.py:167
  439.4 2.4 multiply_reduce_fusion
  (55 shorter events, 0.6 us)
Async XLA Ops:
  7.2 40.6 %all-reduce.5.cloned.1.call-start = ((), (), s32[]{:S(2)}) async-start(), calls=%async_computation.4 | async-start | bytes 524288 | tf_op jit(solution)/shard_map/psum | solution.py:22
  9.3 4.9 %collective-permute-start = (bf16[128,128]{1,0:T(8,128)(2,1)S(1)}, bf16[128,128]{1,0:T(8,128)(2,1)S(1)}, u32[]{:S(2)}, u32[]{:S(2)}) collective-permute-start(bf16[128,128]{1,0:T(8,128)(2,1)S(1)} %copy.41), channel_id=1, source_target_pairs={{0,16},{16,0},{1,17},{17,1},{2,18},{18,2},{3,19},{19,3},{4,20},{20... | collective-permute-start | bytes 98312 | tf_op jit(solution)/shard_map/while/body/eval_jaxpr/ppermute | solution.py:17
  12.3 3.9 collective-permute-start.1
  16.2 3.9 collective-permute-start
  16.6 3.9 collective-permute-start.1
  22.0 235.1 %reduce-scatter.3.cloned.1.call-start = ((), (), s32[]{:S(2)}) async-start(), calls=%async_computation.2 | async-start | bytes 17825792 | tf_op jit(solution)/shard_map/reduce_scatter | solution.py:166
  47.8 21.2 %copy-start.2 = (bf16[128,512]{1,0:T(8,128)(2,1)S(1)}, bf16[128,512]{1,0:T(8,128)(2,1)}, u32[]{:S(2)}) copy-start(bf16[128,512]{1,0:T(8,128)(2,1)} %get-tuple-element.838) | copy-start | bytes 393220
  69.0 370.4 %reduce-scatter.5.cloned.1.call-start = ((), (), s32[]{:S(2)}) async-start(), calls=%async_computation.3 | async-start | bytes 17825792 | tf_op jit(solution)/shard_map/reduce_scatter | solution.py:167
  69.0 24.8 %copy-start.1 = (bf16[128,512]{1,0:T(8,128)(2,1)S(1)}, bf16[128,512]{1,0:T(8,128)(2,1)}, u32[]{:S(2)}) copy-start(bf16[128,512]{1,0:T(8,128)(2,1)} %param.14) | copy-start | bytes 393220
  69.0 75.9 %copy-start = (bf16[128,512]{0,1:T(8,128)(2,1)S(1)}, bf16[128,512]{0,1:T(8,128)(2,1)}, u32[]{:S(2)}) copy-start(bf16[128,512]{0,1:T(8,128)(2,1)} %get-tuple-element.839) | copy-start | bytes 393220
  69.1 370.3 %copy-start.3 = (f32[2048]{0:T(1024)S(1)}, f32[2048]{0:T(1024)}, u32[]{:S(2)}) copy-start(f32[2048]{0:T(1024)} %param.16) | copy-start | bytes 24580
  94.3 5.4 %collective-permute-start.3 = (bf16[128,128]{1,0:T(8,128)(2,1)S(1)}, bf16[128,128]{1,0:T(8,128)(2,1)S(1)}, u32[]{:S(2)}, u32[]{:S(2)}) collective-permute-start(bf16[128,128]{1,0:T(8,128)(2,1)S(1)} %copy.60), channel_id=1, source_target_pairs={{0,16},{16,0},{1,17},{17,1},{2,18},{18,2},{3,19},{19,3},{4,20},{20... | collective-permute-start | bytes 98312 | tf_op jit(solution)/shard_map/while/body/eval_jaxpr/ppermute | solution.py:17
  94.6 5.2 %collective-permute-start.2 = (bf16[128,128]{1,0:T(8,128)(2,1)S(1)}, bf16[128,128]{1,0:T(8,128)(2,1)S(1)}, u32[]{:S(2)}, u32[]{:S(2)}) collective-permute-start(bf16[128,128]{1,0:T(8,128)(2,1)S(1)} %copy.59), channel_id=1, source_target_pairs={{0,16},{16,0},{1,17},{17,1},{2,18},{18,2},{3,19},{19,3},{4,20},{20... | collective-permute-start | bytes 98312 | tf_op jit(solution)/shard_map/while/body/eval_jaxpr/ppermute | solution.py:17
  97.1 4.3 collective-permute-start.4
  97.5 4.6 %collective-permute-start.5 = (f32[128,128]{1,0:T(8,128)S(1)}, f32[128,128]{1,0:T(8,128)S(1)}, u32[]{:S(2)}, u32[]{:S(2)}) collective-permute-start(f32[128,128]{1,0:T(8,128)S(1)} %fusion.116), channel_id=1, source_target_pairs={{0,16},{16,0},{1,17},{17,1},{2,18},{18,2},{3,19},{19,3},{4,20},{20... | collective-permute-start | bytes 196616 | tf_op jit(solution)/shard_map/while/body/eval_jaxpr/ppermute | solution.py:17
  102.2 5.3 %collective-permute-start.3 = (bf16[128,128]{1,0:T(8,128)(2,1)S(1)}, bf16[128,128]{1,0:T(8,128)(2,1)S(1)}, u32[]{:S(2)}, u32[]{:S(2)}) collective-permute-start(bf16[128,128]{1,0:T(8,128)(2,1)S(1)} %copy.60), channel_id=1, source_target_pairs={{0,16},{16,0},{1,17},{17,1},{2,18},{18,2},{3,19},{19,3},{4,20},{20... | collective-permute-start | bytes 98312 | tf_op jit(solution)/shard_map/while/body/eval_jaxpr/ppermute | solution.py:17
  103.7 3.9 collective-permute-start.2
  104.9 4.3 collective-permute-start.4
  106.7 4.3 collective-permute-start.5
Sparse Core Ops, SparseCore 0:
  22.1 25.6 all-reduce.4
  69.1 187.9 reduce-scatter.2
  261.8 177.5 reduce-scatter.4
where the time goes:
time: 449 us; the launch traced here: 448 us
  waiting for transfers between devices  298 us (66%)
  blocking collectives  65.5 us (15%)
  matrix products  49.3 us (11%)
  between operations  13.9 us (3%)
  starting transfers between devices  13.7 us (3%)
  other arithmetic  5.2 us (1%)
    reduce_scatter x1, waiting for transfers between devices, body(): lax.psum_scatter(attrib_part, ('section', 'tp'), scatter_dimension=1, til...  182 us
    reduce_scatter x1, waiting for transfers between devices, body(): lax.psum_scatter(encoded_part, ('section', 'tp'), scatter_dimension=1, ti...  79.6 us
    psum x1, blocking collectives, body(): key_sum, value_sum = lax.psum((key_full, value_full), 'tp')  33 us
    psum x1, blocking collectives, body(): squares = lax.psum(jnp.sum(wide_out * wide_out, axis=1), ('section', 'tp'))  32.5 us
    psum x1, waiting for transfers between devices, spread(): return lax.psum(jnp.where(mine, value, jnp.zeros_like(value)), axis)  25.8 us
    dot_general x1, matrix products, body(): lax.dot_general(scored_grad, dec_weight, (((1,), (1,)), ((), ())), prefer...  24.8 us
    dot_general x1, matrix products, body(): jnp.dot(scored_out, enc_weight, preferred_element_type=jnp.float32)  21.1 us
    ppermute x12, starting transfers between devices, passed_along(): return lax.ppermute(value, axis, pairs)  13.6 us
  transfers between devices with their start and end apart: 15, of which 12 were waited for; matrix products, arithmetic and copies ran while one was open for 7% of the time, Pallas kernels for 0%

commit v1 on v0

--- a/solution.py
+++ b/solution.py
@@ -3,6 +3,7 @@
 import jax.numpy as jnp
 from jax import lax
 from jax.sharding import PartitionSpec as P
+from jax.lax import all_gather
 
 QUERY_HEADS = 64
 KEY_VALUE_HEADS = 8
@@ -19,7 +20,8 @@
 
 def spread(value, axis, root):
     mine = lax.axis_index(axis) == root
-    return lax.psum(jnp.where(mine, value, jnp.zeros_like(value)), axis)
+    fill_target = lambda frame_in, group_axis: jnp.sum(all_gather(frame_in, group_axis), axis=0)
+    return fill_target(jnp.where(mine, value, jnp.zeros_like(value)), axis)
 
 
 def token_positions(device, row_count, cycle_size):

time: 449 us -> 428 us (0.953)
  waiting for transfers between devices: 298 us -> 265 us
  blocking collectives: 65.5 us -> 77.2 us
    psum x1 -> x0, waiting for transfers between devices: 25.8 us -> none  [spread(): return lax.psum(jnp.where(mine, value, jnp.zeros_like(value)), axis)]
    all_gather x0 -> x2, blocking collectives: none -> 11.3 us  [spread(): all_gather(frame_in, group_axis)]
    reduce_scatter x1, waiting for transfers between devices: 79.6 us -> 73.1 us  [body(): lax.psum_scatter(encoded_part, ('section', 'tp'), scatter_dimension=1, ti...]
  transfers between devices with their start and end apart: 15 -> 14, of which waited for: 12 -> 11; matrix products, arithmetic and copies ran while one was open for 7% -> 7% of each run, Pallas kernels for 0% -> 0%
where the time goes in v1:
time: 428 us
  waiting for transfers between devices  265 us (62%)
  blocking collectives  77.2 us (18%)
  matrix products  50.5 us (12%)
  between operations  14.3 us (3%)
  starting transfers between devices  13.7 us (3%)
    reduce_scatter x1, waiting for transfers between devices, body(): lax.psum_scatter(attrib_part, ('section', 'tp'), scatter_dimension=1, til...  182 us
    reduce_scatter x1, waiting for transfers between devices, body(): lax.psum_scatter(encoded_part, ('section', 'tp'), scatter_dimension=1, ti...  73.1 us
    psum x1, blocking collectives, body(): squares = lax.psum(jnp.sum(wide_out * wide_out, axis=1), ('section', 'tp'))  34.3 us
    psum x1, blocking collectives, body(): key_sum, value_sum = lax.psum((key_full, value_full), 'tp')  31.6 us
    dot_general x1, matrix products, body(): lax.dot_general(scored_grad, dec_weight, (((1,), (1,)), ((), ())), prefer...  26.3 us
    dot_general x1, matrix products, body(): jnp.dot(scored_out, enc_weight, preferred_element_type=jnp.float32)  20.8 us
    ppermute x12, starting transfers between devices, passed_along(): return lax.ppermute(value, axis, pairs)  13.6 us
    all_gather x2, blocking collectives, spread(): all_gather(frame_in, group_axis)  11.3 us
  transfers between devices with their start and end apart: 14, of which 11 were waited for; matrix products, arithmetic and copies ran while one was open for 7% of the time, Pallas kernels for 0%

profile of v1, /device:TPU:0, one launch (start us, length us, event | category | flops | bytes accessed | tf_op | source)
XLA Modules:
  0.0 427.7 jit_solution(4431521242133067180)
XLA Ops:
  7.3 0.8 constant_dynamic-slice_fusion
  8.1 1.0 copy.28
  9.1 0.1 copy.32
  9.2 11.2 %while.54 = (s32[]{:T(128)}, bf16[128,128]{1,0:T(8,128)(2,1)S(1)}, bf16[128,128]{1,0:T(8,128)(2,1)S(1)}, f32[4,128]{1,0:T(4,128)S(1)}, f32[4,128]{1,0:T(4,128)S(...) while((s32[]{:T(128)}, bf16[128,128]{1,0:T(8,128)(2,1)S(1)}, ...), condition=%wide.region_3.4_spmd.clone.clone.clone, body=%wide.region_0.3_spmd.clone.clone.clone.sunk | while | flops 51598352 | bytes 2838894 | solution.py:100
  9.3 3.0 collective-permute-start
  12.3 0.1 collective-permute-start.1
  12.4 0.1 broadcast_compare_fusion.4
  12.5 0.2 fusion.96
  12.7 0.1 fusion.97
  12.8 0.2 fusion.99
  13.0 0.3 fusion.100
  13.3 0.9 collective-permute-done
  14.2 2.0 collective-permute-done.1
  16.2 0.3 collective-permute-start
  16.6 1.7 collective-permute-start.1
  18.3 0.1 broadcast_compare_fusion.4
  18.4 0.2 fusion.96
  18.7 0.2 fusion.99
  18.9 0.3 fusion.100
  19.2 1.0 collective-permute-done
  20.1 0.4 collective-permute-done.1
  20.5 0.1 copy.31
  20.7 0.1 copy.35
  20.8 5.6 %all_gather.10 = bf16[2,128,512]{2,1,0:T(8,128)(2,1)S(1)} all-gather(bf16[1,128,512]{2,1,0:T(8,128)(2,1)S(1)} %copy.35), channel_id=1, replica_groups=mesh['ctx'=2,'section'=4,'tp'=4] {'ctx'}, dimensions={0}, use_global_device_ids=true | all-gather | bytes 393216 | tf_op jit(solution)/shard_map/all_gather | solution.py:23
  26.5 20.8 %fusion.48 = f32[128,32768]{1,0:T(8,128)} fusion(bf16[128,512]{1,0:T(8,128)(2,1)S(1)} %reduce_sum.69, bf16[512,32768]{1,0:T(8,128)(2,1)} %param.15), kind=kOutput, calls=%fused_computation.83 | convolution fusion | flops 4294967296 | bytes 50462720 | tf_op jit(solution)/shard_map/dot_general | solution.py:163
  47.4 5.6 %all-gather = bf16[256,512]{1,0:T(8,128)(2,1)S(1)} all-gather(bf16[128,512]{1,0:T(8,128)(2,1)S(1)} %broadcast_select_fusion), channel_id=2, replica_groups=mesh['ctx'=2,'section'=4,'tp'=4] {'ctx'}, dimensions={0}, use_global_device_ids=true | all-gather | bytes 393216 | tf_op jit(solution)/shard_map/all_gather | solution.py:23
  53.1 26.3 %fusion.49 = f32[128,32768]{1,0:T(8,128)} fusion(bf16[128,512]{1,0:T(8,128)(2,1)S(1)} %reduce_sum.71, bf16[32768,512]{1,0:T(8,128)(2,1)} %param.17), kind=kOutput, calls=%fused_computation.84 | convolution fusion | flops 4294967296 | bytes 50462720 | tf_op jit(solution)/shard_map/dot_general | solution.py:164
  79.5 0.1 copy.30
  79.6 0.1 copy.40
  79.8 0.1 copy.33
  80.0 0.1 broadcast_bitcast_fusion
  80.1 16.8 %while.55 = (s32[]{:T(128)}, bf16[128,128]{1,0:T(8,128)(2,1)S(1)}, bf16[128,128]{1,0:T(8,128)(2,1)S(1)}, f32[128,128]{1,0:T(8,128)S(1)}, f32[128,128]{1,0:T(8,12...) while((s32[]{:T(128)}, bf16[128,128]{1,0:T(8,128)(2,1)S(1)}, ...), condition=%wide.region_6.7_spmd.clone.clone.clone, body=%wide.region_5.6_spmd.clone.clone.clone.sunk | while | flops 84527632 | bytes 3545556 | solution.py:140
  80.1 1.7 collective-permute-start.3
  81.8 0.4 collective-permute-start.2
  82.2 0.1 broadcast_compare_fusion.5
  82.3 0.2 fusion.113
  82.5 0.2 fusion.114
  82.7 0.2 fusion.115
  82.9 1.7 collective-permute-start.4
  84.6 0.2 fusion.116
  84.8 0.5 collective-permute-start.5
  85.3 0.2 fusion.117
  85.5 0.5 collective-permute-done.2
  86.0 1.4 collective-permute-done.4
  87.4 1.7 collective-permute-done.5
  89.1 0.5 collective-permute-start.3
  89.6 1.6 collective-permute-start.2
  91.2 0.1 broadcast_compare_fusion.5
  91.3 0.2 fusion.113
  91.5 0.2 fusion.114
  91.7 0.2 fusion.115
  91.9 0.5 collective-permute-start.4
  92.4 0.2 fusion.116
  92.6 1.6 collective-permute-start.5
  94.2 0.2 fusion.117
  94.5 1.7 collective-permute-done.4
  96.2 0.7 collective-permute-done.5
  97.1 0.1 multiply_reduce_fusion.1
  97.1 34.3 %psum.23 = f32[128]{0:T(128)S(1)} all-reduce(f32[128]{0:T(128)S(1)} %multiply_reduce_fusion.1), channel_id=1, replica_groups=mesh['ctx'=2,'section'=4,'tp'=4] {'section','tp'}, use_global_device_ids=true, to_apply=%region_12.13 | all-reduce | flops 128 | bytes 1024 | tf_op jit(solution)/shard_map/psum | solution.py:161
  131.4 31.6 %all-reduce.2 = (bf16[128,256]{1,0:T(8,128)(2,1)}, bf16[128,256]{1,0:T(8,128)(2,1)}) all-reduce(f32[128,256]{1,0:T(8,128)S(1)} %get-tuple-element.864, f32[128,256]{1,0:T(8,128)S(1)} %get-tuple-element.863), channel_id=1, replica_groups=mesh['ctx'=2,'section'=4,'tp'=4] {'tp'}, use_global_device_ids=true, to_apply=%region_7.8 | all-reduce | flops 65536 | bytes 393216 | tf_op jit(solution)/shard_map/psum | solution.py:154
  163.0 0.7 copy_bitcast_fusion
  163.7 73.1 %reduce-scatter.3.cloned.1.call-done = f32[128,2048]{1,0:T(8,128)} async-done(((f32[128,32768]{1,0:T(8,128)}), f32[128,2048]{1,0:T(8,128)}) %reduce-scatter.3.cloned.1.call-update) | async-done | bytes 1048592 | tf_op jit(solution)/shard_map/reduce_scatter | solution.py:168
  236.8 181.7 %reduce-scatter.5.cloned.1.call-done = f32[128,2048]{1,0:T(8,128)} async-done(((f32[128,32768]{1,0:T(8,128)}), f32[128,2048]{1,0:T(8,128)}) %reduce-scatter.5.cloned.1.call-update) | async-done | bytes 1048592 | tf_op jit(solution)/shard_map/reduce_scatter | solution.py:169
  418.5 2.4 multiply_reduce_fusion
  (54 shorter events, 0.7 us)
Async XLA Ops:
  7.2 229.6 %reduce-scatter.3.cloned.1.call-start = ((), (), s32[]{:S(2)}) async-start(), calls=%async_computation.2 | async-start | bytes 17825792 | tf_op jit(solution)/shard_map/reduce_scatter | solution.py:168
  9.3 4.9 %collective-permute-start = (bf16[128,128]{1,0:T(8,128)(2,1)S(1)}, bf16[128,128]{1,0:T(8,128)(2,1)S(1)}, u32[]{:S(2)}, u32[]{:S(2)}) collective-permute-start(bf16[128,128]{1,0:T(8,128)(2,1)S(1)} %copy.54), channel_id=1, source_target_pairs={{0,16},{16,0},{1,17},{17,1},{2,18},{18,2},{3,19},{19,3},{4,20},{20... | collective-permute-start | bytes 98312 | tf_op jit(solution)/shard_map/while/body/eval_jaxpr/ppermute | solution.py:18
  12.3 3.9 collective-permute-start.1
  16.2 3.9 collective-permute-start
  16.6 3.9 collective-permute-start.1
  26.5 20.9 %copy-start = (bf16[128,512]{1,0:T(8,128)(2,1)S(1)}, bf16[128,512]{1,0:T(8,128)(2,1)}, u32[]{:S(2)}) copy-start(bf16[128,512]{1,0:T(8,128)(2,1)} %param.14) | copy-start | bytes 393220
  47.4 371.1 %reduce-scatter.5.cloned.1.call-start = ((), (), s32[]{:S(2)}) async-start(), calls=%async_computation.3 | async-start | bytes 17825792 | tf_op jit(solution)/shard_map/reduce_scatter | solution.py:169
  53.1 365.3 %copy-start.1 = (f32[2048]{0:T(1024)S(1)}, f32[2048]{0:T(1024)}, u32[]{:S(2)}) copy-start(f32[2048]{0:T(1024)} %param.16) | copy-start | bytes 24580
  80.1 5.4 %collective-permute-start.3 = (bf16[128,128]{1,0:T(8,128)(2,1)S(1)}, bf16[128,128]{1,0:T(8,128)(2,1)S(1)}, u32[]{:S(2)}, u32[]{:S(2)}) collective-permute-start(bf16[128,128]{1,0:T(8,128)(2,1)S(1)} %copy.73), channel_id=1, source_target_pairs={{0,16},{16,0},{1,17},{17,1},{2,18},{18,2},{3,19},{19,3},{4,20},{20... | collective-permute-start | bytes 98312 | tf_op jit(solution)/shard_map/while/body/eval_jaxpr/ppermute | solution.py:18
  81.8 4.2 collective-permute-start.2
  82.9 4.5 %collective-permute-start.4 = (f32[128,128]{1,0:T(8,128)S(1)}, f32[128,128]{1,0:T(8,128)S(1)}, u32[]{:S(2)}, u32[]{:S(2)}) collective-permute-start(f32[128,128]{1,0:T(8,128)S(1)} %fusion.115), channel_id=1, source_target_pairs={{0,16},{16,0},{1,17},{17,1},{2,18},{18,2},{3,19},{19,3},{4,20},{20... | collective-permute-start | bytes 196616 | tf_op jit(solution)/shard_map/while/body/eval_jaxpr/ppermute | solution.py:18
  84.8 4.3 %collective-permute-start.5 = (f32[128,128]{1,0:T(8,128)S(1)}, f32[128,128]{1,0:T(8,128)S(1)}, u32[]{:S(2)}, u32[]{:S(2)}) collective-permute-start(f32[128,128]{1,0:T(8,128)S(1)} %fusion.116), channel_id=1, source_target_pairs={{0,16},{16,0},{1,17},{17,1},{2,18},{18,2},{3,19},{19,3},{4,20},{20... | collective-permute-start | bytes 196616 | tf_op jit(solution)/shard_map/while/body/eval_jaxpr/ppermute | solution.py:18
  89.1 5.3 %collective-permute-start.3 = (bf16[128,128]{1,0:T(8,128)(2,1)S(1)}, bf16[128,128]{1,0:T(8,128)(2,1)S(1)}, u32[]{:S(2)}, u32[]{:S(2)}) collective-permute-start(bf16[128,128]{1,0:T(8,128)(2,1)S(1)} %copy.73), channel_id=1, source_target_pairs={{0,16},{16,0},{1,17},{17,1},{2,18},{18,2},{3,19},{19,3},{4,20},{20... | collective-permute-start | bytes 98312 | tf_op jit(solution)/shard_map/while/body/eval_jaxpr/ppermute | solution.py:18
  89.6 4.9 %collective-permute-start.2 = (bf16[128,128]{1,0:T(8,128)(2,1)S(1)}, bf16[128,128]{1,0:T(8,128)(2,1)S(1)}, u32[]{:S(2)}, u32[]{:S(2)}) collective-permute-start(bf16[128,128]{1,0:T(8,128)(2,1)S(1)} %copy.72), channel_id=1, source_target_pairs={{0,16},{16,0},{1,17},{17,1},{2,18},{18,2},{3,19},{19,3},{4,20},{20... | collective-permute-start | bytes 98312 | tf_op jit(solution)/shard_map/while/body/eval_jaxpr/ppermute | solution.py:18
  91.9 4.3 %collective-permute-start.4 = (f32[128,128]{1,0:T(8,128)S(1)}, f32[128,128]{1,0:T(8,128)S(1)}, u32[]{:S(2)}, u32[]{:S(2)}) collective-permute-start(f32[128,128]{1,0:T(8,128)S(1)} %fusion.115), channel_id=1, source_target_pairs={{0,16},{16,0},{1,17},{17,1},{2,18},{18,2},{3,19},{19,3},{4,20},{20... | collective-permute-start | bytes 196616 | tf_op jit(solution)/shard_map/while/body/eval_jaxpr/ppermute | solution.py:18
  92.6 4.3 %collective-permute-start.5 = (f32[128,128]{1,0:T(8,128)S(1)}, f32[128,128]{1,0:T(8,128)S(1)}, u32[]{:S(2)}, u32[]{:S(2)}) collective-permute-start(f32[128,128]{1,0:T(8,128)S(1)} %fusion.116), channel_id=1, source_target_pairs={{0,16},{16,0},{1,17},{17,1},{2,18},{18,2},{3,19},{19,3},{4,20},{20... | collective-permute-start | bytes 196616 | tf_op jit(solution)/shard_map/while/body/eval_jaxpr/ppermute | solution.py:18
Sparse Core Ops, SparseCore 0:
  47.5 189.2 reduce-scatter.2
  240.9 177.5 reduce-scatter.4
